TPU v7x, 256 devices: a whole 4x4x8 slice. The times are simulated.
256 devices in a mesh: dp: 64 (over z_hi, x, y, core), own: 4 (over z_lo).
Axes of the slice: x: 4, y: 4, z: 8 (z_hi: 2, z_lo: 4; z = z_hi * 4 + z_lo), core: 2. Of those that a mesh axis runs over, the one named last changes fastest.
Arguments:
- acts_q: bfloat16 [262144, 512], P(('dp', 'own')), may hold values from -54 to 54
- grads_q: bfloat16 [262144, 384], P(('dp', 'own')), may hold values from -180 to 180
- acts_o: bfloat16 [262144, 384], P(('dp', 'own')), may hold values from -54 to 54
- grads_o: bfloat16 [262144, 512], P(('dp', 'own')), may hold values from -180 to 180
- sample_rows: int32 [4096], P(('dp', 'own')), may hold values from 0 to 1023
- start_aq: float32 [512, 512], replicated, may hold values from -2 to 16, as said below
- start_gq: float32 [384, 384], replicated, may hold values from -2 to 16, as said below
- start_ao: float32 [384, 384], replicated, may hold values from -2 to 16, as said below
- start_go: float32 [512, 512], replicated, may hold values from -2 to 16, as said below
- weight_q: float32 [512, 384], P('dp', 'own'), may hold values from -0.25 to 0.25
- weight_o: float32 [384, 512], P('dp', 'own'), may hold values from -0.3125 to 0.3125
Outputs:
- new_q: float32 [512, 384], replicated
- new_o: float32 [384, 512], replicated
Inputs may be any that keep to these rules, and one draw needn't show every extreme that they name: `start_aq`: symmetric positive definite. `start_gq`: symmetric positive definite. `start_ao`: symmetric positive definite. `start_go`: symmetric positive definite.
All inputs are finite; a program needn't handle non-finite values.
Results may differ from a plain program's by a relative error of at most 0.0008.
Values may be sent and summed in bfloat16 or wider, within the bound.
A program may use at most 128 MiB of HBM per device.

v0:
```python
import jax
import jax.numpy as jnp
from jax import lax
from jax.sharding import PartitionSpec as P

ITERS = 4


DECAY = 0.5
DAMPING = 0.5
LEARNING_RATE = 10.0
FACTOR_OWNERS = (0, 1, 2, 0)


def spread(value, axis, source):
    kept = jnp.where(lax.axis_index(axis) == source, value, 0).astype(value.dtype)
    return lax.psum(kept, axis)


def damped(start, cov):
    width = start.shape[0]
    return DECAY * start + (1.0 - DECAY) * cov + DAMPING * jnp.eye(width, dtype=jnp.float32)


def first_iterate(matrix):
    width = matrix.shape[0]
    scale = 1.0 / jnp.sqrt(jnp.sum(matrix * matrix))
    return scale * jnp.eye(width, dtype=jnp.float32)


def newton(matrix):
    approx = first_iterate(matrix)
    for iteration in range(ITERS):
        product = jnp.dot(matrix, approx, precision=lax.Precision.HIGHEST)
        approx = 2.0 * approx - jnp.dot(product, approx, precision=lax.Precision.HIGHEST)
    return approx


def outer_sum(sampled):
    return jnp.einsum("ti,tj->ij", sampled, sampled, preferred_element_type=jnp.float32)


def per_device(
    acts_q,
    grads_q,
    acts_o,
    grads_o,
    sample_rows,
    start_aq,
    start_gq,
    start_ao,
    start_go,
    weight_q,
    weight_o,
):
    group_count = lax.axis_size("dp") * lax.axis_size("own")
    total_tokens = acts_q.shape[0] * group_count
    total_samples = sample_rows.shape[0] * group_count
    own_index = lax.axis_index("own")
    starts = (start_aq, start_gq, start_ao, start_go)
    picked = (
        jnp.take(acts_q, sample_rows, axis=0),
        jnp.take(grads_q, sample_rows, axis=0),
        jnp.take(acts_o, sample_rows, axis=0),
        jnp.take(grads_o, sample_rows, axis=0),
    )
    local_q = jnp.einsum("ti,tj->ij", acts_q, grads_q, preferred_element_type=jnp.float32)
    local_o = jnp.einsum("ti,tj->ij", acts_o, grads_o, preferred_element_type=jnp.float32)
    summed = lax.psum(
        (
            outer_sum(picked[0]),
            outer_sum(picked[1]),
            outer_sum(picked[2]),
            outer_sum(picked[3]),
            local_q,
            local_o,
        ),
        ("dp", "own"),
    )
    factors = [damped(starts[index], summed[index] / total_samples) for index in range(4)]
    grad_q, grad_o = (summed[4], summed[5])
    grad_q = grad_q / total_tokens
    grad_o = grad_o / total_tokens
    inverses = []
    for factor_index in range(4):
        owner_root = FACTOR_OWNERS[factor_index]
        local_inverse = lax.cond(
            own_index == owner_root, newton, jnp.zeros_like, factors[factor_index]
        )
        inverses.append(spread(local_inverse, "own", owner_root))
    dp_index = lax.axis_index("dp")

    def updated(weight_block, inverse_left, gradient, inverse_right):
        row_len, col_len = weight_block.shape
        left_rows = lax.dynamic_slice_in_dim(inverse_left, dp_index * row_len, row_len, 0)
        right_cols = lax.dynamic_slice_in_dim(inverse_right, own_index * col_len, col_len, 1)
        left = jnp.dot(left_rows, gradient, precision=lax.Precision.HIGHEST)
        return weight_block - LEARNING_RATE * jnp.dot(
            left, right_cols, precision=lax.Precision.HIGHEST
        )

    block_q = updated(weight_q, inverses[0], grad_q, inverses[1])
    block_o = updated(weight_o, inverses[2], grad_o, inverses[3])
    wide_q, wide_o = (
        lax.all_gather(block_q, "own", axis=1, tiled=True),
        lax.all_gather(block_o, "own", axis=1, tiled=True),
    )
    new_q, new_o = (
        lax.all_gather(wide_q, "dp", axis=0, tiled=True),
        lax.all_gather(wide_o, "dp", axis=0, tiled=True),
    )
    return (new_q, new_o)


def solution(mesh):
    return jax.shard_map(
        per_device,
        mesh=mesh,
        in_specs=(
            P(("dp", "own"), None),
            P(("dp", "own"), None),
            P(("dp", "own"), None),
            P(("dp", "own"), None),
            P(("dp", "own")),
            P(),
            P(),
            P(),
            P(),
            P("dp", "own"),
            P("dp", "own"),
        ),
        out_specs=(P(), P()),
        check_vma=False,
    )
```

profile of v0, /device:TPU:1, one launch (start us, length us, event | category | flops | bytes accessed | tf_op | source)
XLA Modules:
  0.0 768.6 jit_solution(2651436532255893562)
XLA Ops:
  7.2 0.0 copy-start
  7.2 0.0 all-reduce.5.cloned.1.call-start
  7.2 0.7 compare_select_fusion
  8.0 0.4 copy-done
  8.4 0.6 gather_fusion
  9.0 1.8 gather_fusion.1
  10.8 0.0 copy-start.5
  10.9 0.0 copy-start.6
  10.9 2.9 fusion.97
  13.8 0.6 gather_fusion.3
  14.4 0.6 gather_fusion.2
  15.0 1.5 fusion.98
  16.4 1.4 fusion.57
  17.8 1.4 fusion.59
  19.2 1.2 fusion.64
  20.4 1.2 fusion.66
  21.5 0.0 all-reduce.5.cloned.1.call-update
  21.6 0.0 all-reduce.7.cloned.1.call-start
  21.7 0.1 fusion.47
  21.8 277.4 %all-reduce.5.cloned.1.call-done = (f32[512,384]{1,0:T(8,128)}, f32[512,512]{1,0:T(8,128)}, f32[384,384]{1,0:T(8,128)}, f32[384,512]{1,0:T(8,128)}, f32[384,384]{1,0:T(8,128)}, /*index=5*/f32[512,512]{1,0:T(8,128)}) async-done(((f32[512,384]{1,0:T(8,128)}, f32[512,512]{1,0:T(8,128)}, f32[384,384]{1,0:T(8,128)}, f32[384,512]{1,0:T(8,128)}, f32[384,384]{1,0:T(8,128)}, /*index=5*/f32[512,512]{1,0:T(8,128)}), ...) | async-done | bytes 4849680 | tf_op jit(solution)/shard_map/psum | solution.py:69
  299.2 0.9 broadcast.92
  300.0 0.4 conditional.5
  300.4 0.8 copy-done.2
  301.2 7.9 %conditional.6 = (f32[384,384]{1,0:T(8,128)}) conditional(s32[]{:T(128)} %convert_element_type.17, () %tuple.42, (f32[384,384]{1,0:T(8,128)}, f32[384,384]{1,0:T(8,128)}, f32[384,384]{1,0:T(8,128)}, f32[384,384]{1,0:T(8,128)S(1)}) %tuple.43), branch_computations={%region_12.15_spmd, %region_13.17_spmd} | conditional | flops 5438767104 | bytes 15925276 | solution.py:87
  301.2 0.9 broadcast.80
  309.1 1.1 broadcast_select_fusion.2
  310.2 1.1 broadcast.90
  311.3 24.6 %conditional.4 = (f32[512,512]{1,0:T(8,128)S(1)}) conditional(s32[]{:T(128)} %convert_element_type.14, () %tuple.38, (f32[512,512]{1,0:T(8,128)}, f32[512,512]{1,0:T(8,128)}, f32[512,512]{1,0:T(8,128)}, f32[512,512]{1,0:T(8,128)S(1)}) %tuple.39), branch_computations={%region_1.3_spmd, %region_2.5_spmd} | conditional | flops 12890144768 | bytes 28311580 | solution.py:87
  311.3 3.0 multiply_reduce_fusion
  315.0 1.9 fusion.2
  316.9 1.9 fusion.4
  318.8 3.5 fusion.85
  322.3 1.8 convolution_subtract_fusion.2
  324.2 3.7 fusion.86
  327.8 1.8 convolution_subtract_fusion.1
  329.7 3.5 fusion.87
  333.2 1.9 convolution_subtract_fusion
  335.9 1.0 copy-done.1
  336.9 23.9 %conditional.7 = (f32[512,512]{1,0:T(8,128)S(1)}) conditional(s32[]{:T(128)} %convert_element_type.14, () %tuple.44, (f32[512,512]{1,0:T(8,128)}, f32[512,512]{1,0:T(8,128)}, f32[512,512]{1,0:T(8,128)}, f32[512,512]{1,0:T(8,128)S(1)}) %tuple.45), branch_computations={%region_18.21_spmd, %region_19.23_spmd} | conditional | flops 12890144768 | bytes 28311580 | solution.py:87
  336.9 3.0 multiply_reduce_fusion.3
  340.6 1.9 fusion.33
  342.5 1.9 fusion.35
  344.4 3.5 fusion.94
  347.9 1.8 convolution_subtract_fusion.13
  349.7 3.6 fusion.95
  353.4 1.8 convolution_subtract_fusion.12
  355.2 3.5 fusion.96
  358.7 1.8 convolution_subtract_fusion.11
  360.8 2.8 broadcast_select_fusion
  363.6 0.0 all-reduce.7.cloned.1.call-update
  363.6 134.9 %all-reduce.7.cloned.1.call-done = (f32[512,512]{1,0:T(8,128)}, f32[384,384]{1,0:T(8,128)}, f32[384,384]{1,0:T(8,128)}, f32[512,512]{1,0:T(8,128)}) async-done(((f32[512,512]{1,0:T(8,128)}, f32[384,384]{1,0:T(8,128)}, f32[384,384]{1,0:T(8,128)}, f32[512,512]{1,0:T(8,128)}), (f32[512,512]{1,0:T(8,128)}, f32[384,384]{1,0:T(8,128)}, f32[384,384]{1,0:T(8,128)}, ...) | async-done | bytes 3276816 | tf_op jit(solution)/shard_map/psum | solution.py:17
  498.5 1.2 fusion.48
  499.7 1.2 fusion.44
  500.9 10.7 %all_gather.14 = f32[6,512]{1,0:T(8,128)S(1)} all-gather(f32[6,128]{1,0:T(8,128)S(1)} %fusion.44), channel_id=1, replica_groups=mesh['dp'=64,'own'=4] {'own'}, dimensions={1}, use_global_device_ids=true | all-gather | bytes 15360 | tf_op jit(solution)/shard_map/all_gather | solution.py:106
  511.6 122.3 %all-gather.1 = f32[64,6,512]{2,1,0:T(8,128)S(1)} all-gather(f32[1,6,512]{2,1,0:T(8,128)S(1)} %bitcast.70), channel_id=1, replica_groups=mesh['dp'=64,'own'=4] {'dp'}, dimensions={0}, use_global_device_ids=true | all-gather | bytes 798720 | tf_op jit(solution)/shard_map/all_gather | solution.py:110
  633.9 1.0 reshape.53
  634.9 0.4 copy-done.3
  635.3 1.2 fusion.50
  636.5 0.0 copy-done.8
  636.5 1.3 fusion.46
  637.8 10.3 %all-gather = f32[4,96,8]{1,2,0:T(8,128)S(1)} all-gather(f32[1,96,8]{1,2,0:T(8,128)S(1)} %fusion.46), channel_id=1, replica_groups=mesh['dp'=64,'own'=4] {'own'}, dimensions={0}, use_global_device_ids=true | all-gather | bytes 15360 | tf_op jit(solution)/shard_map/all_gather | solution.py:105
  648.2 0.1 reshape.51
  648.3 112.4 %all_gather.13 = f32[512,384]{1,0:T(8,128)S(1)} all-gather(f32[8,384]{1,0:T(8,128)S(1)} %bitcast.71), channel_id=1, replica_groups=mesh['dp'=64,'own'=4] {'dp'}, dimensions={0}, use_global_device_ids=true | all-gather | bytes 798720 | tf_op jit(solution)/shard_map/all_gather | solution.py:109
  760.7 0.9 copy.38
  (17 shorter events, 0.1 us)
Async XLA Ops:
  7.2 1.3 copy-start
  7.2 0.8 copy-start.9
  7.2 292.0 %all-reduce.5.cloned.1.call-start = ((), (), s32[]{:S(2)}) async-start(), calls=%async_computation | async-start | bytes 9699328 | tf_op jit(solution)/shard_map/psum | solution.py:69
  10.8 2.9 copy-start.5
  10.9 3.5 copy-start.6
  21.6 476.9 %all-reduce.7.cloned.1.call-start = ((), (), s32[]{:S(2)}) async-start(), calls=%async_computation.1 | async-start | bytes 6553600 | tf_op jit(solution)/shard_map/psum | solution.py:17
  300.4 0.8 copy-start.2
  335.9 1.0 copy-start.1
  363.6 134.9 %copy-start.4 = (f32[384,512]{1,0:T(8,128)S(1)}, f32[384,512]{1,0:T(8,128)}, u32[]{:S(2)}) copy-start(f32[384,512]{1,0:T(8,128)} %get-tuple-element.99) | copy-start | bytes 2359300
  363.6 136.1 %copy-start.7 = (f32[6,128]{1,0:T(8,128)S(1)}, f32[6,128]{1,0:T(8,128)}, u32[]{:S(2)}) copy-start(f32[6,128]{1,0:T(8,128)} %param.33) | copy-start | bytes 9220
  633.9 1.4 copy-start.3
  633.9 2.6 copy-start.8
Sparse Core Ops, SparseCore 0:
  21.7 277.4 all-reduce.4
  363.7 134.7 all-reduce.6
where the time goes:
time: 784 us; the launch traced here: 769 us
  waiting for transfers between devices  412 us (53%)
  blocking collectives  256 us (33%)
  matrix products  54.3 us (7%)
  between operations  14.4 us (2%)
  local copies, waits for them, and re-layouts  11.1 us (1%)
  other arithmetic  10.8 us (1%)
  loops' own time  10 us (1%)
    psum x1, waiting for transfers between devices, per_device(): lax.psum((outer_sum(picked[0]), outer_sum(picked[1]), outer_sum(picked[2]...  277 us
    psum x1, waiting for transfers between devices, spread(): return lax.psum(kept, axis)  135 us
    all_gather x1, blocking collectives, per_device(): lax.all_gather(wide_o, 'dp', axis=0, tiled=True)  122 us
    all_gather x1, blocking collectives, per_device(): lax.all_gather(wide_q, 'dp', axis=0, tiled=True)  112 us
    dot_general x8, matrix products, newton(): product = jnp.dot(matrix, approx, precision=lax.Precision.HIGHEST)  25 us
  transfers between devices with their start and end apart: 2, of which 2 were waited for; matrix products, arithmetic and copies ran while one was open for 0% of the time, Pallas kernels for 0%

commit v1 on v0

v1 whole, which is shorter than its diff:
```python
import functools

import jax
import jax.numpy as jnp
from jax import lax
from jax.experimental import pallas as pl
from jax.experimental.pallas import tpu as pltpu
from jax.sharding import PartitionSpec as P

MESH = pl.DeviceIdType.MESH
F32 = jnp.float32
BF16 = jnp.bfloat16
DECAY = 0.5
DAMPING = 0.5
LEARNING_RATE = 10.0
TOKENS = 262144
SAMPLES = 4096
BIG = 512
SMALL = 384
BLK = 128
PAIRS = [(i, j) for i in range(4) for j in range(i, 4)] + [
    (i, j) for i in range(4, 7) for j in range(i, 7)
]


def lookup(index, table):
    value = jnp.int32(table[0])
    for position in range(1, len(table)):
        value = jnp.where(index == position, jnp.int32(table[position]), value)
    return value


def dot(a, b, dims=((1,), (0,))):
    return lax.dot_general(a, b, (dims, ((), ())), preferred_element_type=F32)


def high_low(value):
    high = value.astype(BF16)
    return high, (value - high.astype(F32)).astype(BF16)


def dot3(a, b, dims=((1,), (0,))):
    return dot(a[0], b[0], dims) + dot(a[0], b[1], dims) + dot(a[1], b[0], dims)


def eye_mask(n):
    return lax.broadcasted_iota(jnp.int32, (n, n), 0) == lax.broadcasted_iota(
        jnp.int32, (n, n), 1
    )


def diagonal(ref, n):
    mask = eye_mask(BLK)
    cols, rows = [], []
    for i in range(n // BLK):
        at = slice(i * BLK, (i + 1) * BLK)
        block = jnp.where(mask, ref[at, at], 0.0)
        cols.append(jnp.sum(block, axis=1, keepdims=True))
        rows.append(jnp.sum(block, axis=0, keepdims=True))
    return cols, jnp.concatenate(rows, axis=1)


def row_eye(i, n):
    return lax.broadcasted_iota(jnp.int32, (BLK, n), 0) + i * BLK == lax.broadcasted_iota(
        jnp.int32, (BLK, n), 1
    )


def newton_step(n, e_ref, p_ref, eb_ref, pb_ref):
    blocks = range(n // BLK)
    e_col, e_row = diagonal(e_ref, n)
    for i in blocks:
        at = slice(i * BLK, (i + 1) * BLK)
        eb_ref[at, :] = jnp.where(row_eye(i, n), 0.0, e_ref[at, :]).astype(BF16)
        pb_ref[at, :] = jnp.where(row_eye(i, n), 0.0, p_ref[at, :]).astype(BF16)
    for i in blocks:
        at = slice(i * BLK, (i + 1) * BLK)
        square = dot(eb_ref[at, :], eb_ref[...])
        rest = e_ref[at, :]
        weight = jnp.where(row_eye(i, n), e_col[i], e_col[i] + e_row)
        e_ref[at, :] = square + weight * rest
    f_col, f_row = diagonal(e_ref, n)
    p_col, _ = diagonal(p_ref, n)
    for i in blocks:
        at = slice(i * BLK, (i + 1) * BLK)
        eb_ref[at, :] = jnp.where(row_eye(i, n), 0.0, e_ref[at, :]).astype(BF16)
    for i in blocks:
        at = slice(i * BLK, (i + 1) * BLK)
        product = dot(pb_ref[at, :], eb_ref[...])
        p_rows = p_ref[at, :]
        off = jnp.where(row_eye(i, n), 0.0, e_ref[at, :])
        p_ref[at, :] = p_rows + product + p_col[i] * off + p_rows * f_row


def kernel(
    acts_q, grads_q, acts_o, grads_o, rows_ref,
    start_aq, start_gq, start_ao, start_go, wq_ref, wo_ref,
    new_q, new_o,
    mine_b, mine_s, oth_b, oth_s, st_b, st_s,
    g_send, g_mine, g_core, g_y, g_ysum, g_x, g_xsum, g_z, g_full,
    s_send, s_core, s_all,
    c_part, c_y, c_ysum, c_z, c_blocks,
    w_send, w_all,
    e_b, p_b, eb_b, pb_b, e_s, p_s, eb_s, pb_s, m_ref,
    in_sem, send_sem, recv_sem,
):
    dp, own = lax.axis_index("dp"), lax.axis_index("own")
    core = lax.rem(dp, 2)
    y = lax.rem(dp // 2, 4)
    x = lax.rem(dp // 8, 4)
    z = (dp // 32) * 4 + own

    def device(cx, cy, cz, cc):
        return ((cz // 4) * 32 + cx * 8 + cy * 2 + cc, lax.rem(cz, 4))

    partner = device(x, y, z, 1 - core)
    x_peer = [device(lax.rem(x + d, 4), y, z, core) for d in range(4)]
    y_peer = [device(x, lax.rem(y + d, 4), z, core) for d in range(4)]
    z_peer = [device(x, y, lax.rem(z + d, 8), core) for d in range(8)]

    def fetch(src, dst, sem):
        return pltpu.make_async_copy(src, dst, in_sem.at[sem])

    @pl.when(core == 0)
    def _():
        fetch(acts_q, mine_b, 0).start()
        fetch(grads_q, mine_s, 1).start()
        fetch(grads_o, oth_b, 2).start()
        fetch(acts_o, oth_s, 3).start()
        fetch(start_aq, st_b, 4).start()
        fetch(start_gq, st_s, 5).start()

    @pl.when(core == 1)
    def _():
        fetch(grads_o, mine_b, 0).start()
        fetch(acts_o, mine_s, 1).start()
        fetch(acts_q, oth_b, 2).start()
        fetch(grads_q, oth_s, 3).start()
        fetch(start_go, st_b, 4).start()
        fetch(start_ao, st_s, 5).start()

    barrier = pltpu.get_barrier_semaphore()
    for peer in [partner] + x_peer[1:] + y_peer[1:] + z_peer[1:]:
        pl.semaphore_signal(barrier, inc=1, device_id=peer, device_id_type=MESH)

    def remote(src, dst, slot, peer):
        return pltpu.make_async_remote_copy(
            src_ref=src, dst_ref=dst, send_sem=send_sem.at[slot],
            recv_sem=recv_sem.at[slot], device_id=peer, device_id_type=MESH,
        )

    pending = []

    def send(src, dst, slot, peer):
        copy = remote(src, dst, slot, peer)
        copy.start()
        pending.append(copy)
        return copy

    w_send[...] = jnp.zeros_like(w_send)

    @pl.when(core == 0)
    def _():
        w_all[x, y, z, 0] = jnp.zeros((8, BLK), F32)
        w_all[x, y, z, 0, :, 0:96] = wq_ref[...]
        w_send[0:6, :] = wo_ref[...]

    @pl.when(core == 1)
    def _():
        w_all[x, y, z, 1] = jnp.zeros((8, BLK), F32)
        w_all[x, y, z, 1, 0:6, :] = wo_ref[...]
        w_send[:, 0:96] = wq_ref[...]

    fetch(acts_q, oth_b, 2).wait()
    fetch(grads_q, oth_s, 3).wait()
    fetch(acts_q, mine_b, 0).wait()
    fetch(grads_q, mine_s, 1).wait()

    target = jnp.zeros((16, 1024), jnp.int32)
    row = lax.broadcasted_iota(jnp.int32, (16, 1024), 0)
    for k in range(16):
        target = jnp.where(row == k, rows_ref[k], target)
    pick = lax.broadcasted_iota(jnp.int32, (16, 1024), 1) == target
    one_hot = jnp.where(pick, 1.0, 0.0).astype(BF16)

    def sampled(big, small):
        return jnp.concatenate([dot(one_hot, big[...]), dot(one_hot, small[...])], axis=1).astype(BF16)

    picked = sampled(oth_b, oth_s)
    for b in range(7):
        s_send[b] = picked[:, b * BLK : (b + 1) * BLK]
    picked = sampled(mine_b, mine_s)
    for b in range(7):
        s_all[x, b, pl.ds(pl.multiple_of(core * 16, 16), 16), :] = picked[:, b * BLK : (b + 1) * BLK]

    pl.semaphore_wait(barrier, 14)

    slot = 0
    s_copy = send(s_send, s_core, slot, partner)
    slot += 1
    w_copy = send(w_send, w_all.at[x, y, z, core], slot, partner)
    slot += 1

    g_copies = []
    for d in (1, 2, 3, 0):
        c = lax.rem(y + d, 4)
        cols = pl.ds(pl.multiple_of(c * BLK, BLK), BLK)
        g_send[d] = dot(oth_b[:, cols], oth_s[...], ((0,), (0,)))
        g_copies.append(send(g_send.at[d], g_core.at[d], slot, partner))
        slot += 1
        g_mine[d] = dot(mine_b[:, cols], mine_s[...], ((0,), (0,)))

    s_copy.wait_recv()
    for b in range(7):
        s_all[x, b, pl.ds(pl.multiple_of((1 - core) * 16, 16), 16), :] = s_core[b]
    s_copies = []
    for d in (1, 2, 3):
        s_copies.append(send(s_all.at[x], s_all.at[x], slot, x_peer[d]))
        slot += 1

    gy_copies = []
    for index, d in enumerate((1, 2, 3, 0)):
        g_copies[index].wait_recv()
        total = g_mine[d] + g_core[d]
        if d == 0:
            g_y[y] = total
        else:
            g_mine[d] = total
            gy_copies.append(send(g_mine.at[d], g_y.at[y], slot, y_peer[d]))
            slot += 1

    w_copy.wait_recv()
    w_copies = []
    for d in range(1, 8):
        w_copies.append(send(w_all.at[x, y, z], w_all.at[x, y, z], slot, z_peer[d]))
        slot += 1

    for copy in s_copies:
        copy.wait_recv()
    cy_copies = []
    for d in (1, 2, 3, 0):
        block = x * 4 + lax.rem(y + d, 4)
        left = lookup(block, [i for i, _ in PAIRS])
        right = lookup(block, [j for _, j in PAIRS])
        lhs = s_all[:, left].reshape(128, BLK)
        rhs = s_all[:, right].reshape(128, BLK)
        value = dot(lhs, rhs, ((0,), (0,)))
        if d == 0:
            c_y[y] = value
        else:
            c_part[d] = value
            cy_copies.append(send(c_part.at[d], c_y.at[y], slot, y_peer[d]))
            slot += 1

    for copy in w_copies:
        copy.wait_recv()
    w_copies = []
    for d in (1, 2, 3):
        w_copies.append(send(w_all.at[x, y], w_all.at[x, y], slot, y_peer[d]))
        slot += 1

    for copy in cy_copies:
        copy.wait_recv()
    c_ysum[...] = (c_y[0] + c_y[1]) + (c_y[2] + c_y[3])
    cz_copies = []
    for d in range(1, 8):
        rows = pl.ds(pl.multiple_of(lax.rem(z + d, 4) * 32, 32), 32)
        cz_copies.append(send(c_ysum.at[rows], c_z.at[z], slot, z_peer[d]))
        slot += 1
    c_z[z] = c_ysum[pl.ds(pl.multiple_of(own * 32, 32), 32), :]

    for copy in gy_copies:
        copy.wait_recv()
    g_ysum[...] = (g_y[0] + g_y[1]) + (g_y[2] + g_y[3])
    gx_copies = []
    for d in (1, 2, 3):
        rows = pl.ds(pl.multiple_of(lax.rem(x + d, 4) * 32, 32), 32)
        gx_copies.append(send(g_ysum.at[rows], g_x.at[x], slot, x_peer[d]))
        slot += 1
    g_x[x] = g_ysum[pl.ds(pl.multiple_of(x * 32, 32), 32), :]

    for copy in w_copies:
        copy.wait_recv()
    w_copies = []
    for d in (1, 2, 3):
        w_copies.append(send(w_all.at[x], w_all.at[x], slot, x_peer[d]))
        slot += 1

    my_block = x * 4 + y
    for copy in cz_copies:
        copy.wait_recv()
    total = c_z[0]
    for k in range(1, 8):
        total = total + c_z[k]
    c_rows = pl.ds(pl.multiple_of(own * 32, 32), 32)
    c_blocks[my_block, c_rows, :] = total
    cag_copies = []
    for d in (1, 7, 6):
        view = c_blocks.at[my_block, c_rows]
        cag_copies.append(send(view, view, slot, z_peer[d]))
        slot += 1

    for copy in gx_copies:
        copy.wait_recv()
    g_xsum[...] = (g_x[0] + g_x[1]) + (g_x[2] + g_x[3])
    gz_copies = []
    for d in range(1, 8):
        rows = pl.ds(pl.multiple_of(lax.rem(z + d, 4) * 8, 8), 8)
        gz_copies.append(send(g_xsum.at[rows], g_z.at[z], slot, z_peer[d]))
        slot += 1
    g_z[z] = g_xsum[pl.ds(pl.multiple_of(own * 8, 8), 8), :]

    for copy in cag_copies:
        copy.wait_recv()
    cag_copies = []
    for d in (1, 2, 3):
        view = c_blocks.at[my_block]
        cag_copies.append(send(view, view, slot, y_peer[d]))
        slot += 1

    for copy in gz_copies:
        copy.wait_recv()
    total = g_z[0]
    for k in range(1, 8):
        total = total + g_z[k]
    base = y * 128 + x * 32
    g_rows = pl.ds(pl.multiple_of(base + own * 8, 8), 8)
    g_full[g_rows, :] = total
    gag_copies = []
    for d in (1, 7, 6):
        gag_copies.append(send(g_full.at[g_rows], g_full.at[g_rows], slot, z_peer[d]))
        slot += 1

    for copy in cag_copies:
        copy.wait_recv()
    cag_copies = []
    for d in (1, 2, 3):
        view = c_blocks.at[pl.ds(x * 4, 4)]
        cag_copies.append(send(view, view, slot, x_peer[d]))
        slot += 1

    for copy in gag_copies:
        copy.wait_recv()
    gag_copies = []
    g_rows = pl.ds(pl.multiple_of(base, 32), 32)
    for d in (1, 2, 3):
        gag_copies.append(send(g_full.at[g_rows], g_full.at[g_rows], slot, x_peer[d]))
        slot += 1
    for copy in gag_copies:
        copy.wait_recv()
    gag_copies = []
    g_rows = pl.ds(pl.multiple_of(y * 128, 128), 128)
    for d in (1, 2, 3):
        gag_copies.append(send(g_full.at[g_rows], g_full.at[g_rows], slot, y_peer[d]))
        slot += 1

    for copy in w_copies:
        copy.wait_recv()

    @pl.when(core == 0)
    def _():
        def place(step, carry):
            wx, wy = step // 4, lax.rem(step, 4)
            for zh in range(2):
                for cc in range(2):
                    row = pl.multiple_of(((zh * 4 + wx) * 4 + wy) * 16 + cc * 8, 8)
                    for o in range(4):
                        new_q[pl.ds(row, 8), o * 96 : (o + 1) * 96] = w_all[
                            wx, wy, zh * 4 + o, cc, :, 0:96
                        ]
            return carry

        lax.fori_loop(0, 16, place, 0)

    @pl.when(core == 1)
    def _():
        def place(step, carry):
            zh, wx = step // 4, lax.rem(step, 4)
            row = pl.multiple_of(step * 48, 8)
            for o in range(4):
                parts = [
                    w_all[wx, wy, zh * 4 + o, cc, 0:6, :] for wy in range(4) for cc in range(2)
                ]
                new_o[pl.ds(row, 48), o * BLK : (o + 1) * BLK] = jnp.concatenate(parts, axis=0)
            return carry

        lax.fori_loop(0, 8, place, 0)

    fetch(start_aq, st_b, 4).wait()
    fetch(start_gq, st_s, 5).wait()
    for copy in cag_copies:
        copy.wait_recv()

    def factor(n, offset, st_ref, e_ref, p_ref):
        count = n // BLK
        where = {pair: position for position, pair in enumerate(PAIRS)}
        squares = jnp.zeros((1, 1), F32)
        for i in range(count):
            for j in range(i, count):
                block = c_blocks[where[(i + offset, j + offset)]] * (1.0 / SAMPLES)
                for a, b, value in ((i, j, block), (j, i, block.T)) if i != j else ((i, j, block),):
                    at = (slice(a * BLK, (a + 1) * BLK), slice(b * BLK, (b + 1) * BLK))
                    mixed = DECAY * st_ref[at] + (1.0 - DECAY) * value
                    if a == b:
                        mixed = mixed + jnp.where(eye_mask(BLK), DAMPING, 0.0)
                    e_ref[at] = mixed
                    row = jnp.sum(mixed * mixed, axis=0, keepdims=True)
                    squares = squares + jnp.sum(row, axis=1, keepdims=True)
        scale = 1.0 / jnp.sqrt(squares)
        for i in range(count):
            at = slice(i * BLK, (i + 1) * BLK)
            one = jnp.where(row_eye(i, n), 1.0, 0.0)
            rest = one - scale * e_ref[at, :]
            e_ref[at, :] = rest
            p_ref[at, :] = scale * (one + rest)

    factor(BIG, 0, st_b, e_b, p_b)
    factor(SMALL, 4, st_s, e_s, p_s)

    def iterate(step, carry):
        newton_step(BIG, e_b, p_b, eb_b, pb_b)
        newton_step(SMALL, e_s, p_s, eb_s, pb_s)
        return carry

    lax.fori_loop(0, 3, iterate, 0)

    for copy in gag_copies:
        copy.wait_recv()
    grad = high_low(g_full[...] * (1.0 / TOKENS))
    for i in range(4):
        at = slice(i * BLK, (i + 1) * BLK)
        m_ref[at, :] = dot3(high_low(p_b[at, :]), grad)

    @pl.when(core == 0)
    def _():
        right = high_low(p_s[...])
        for i in range(4):
            at = slice(i * BLK, (i + 1) * BLK)
            new_q[at, :] = new_q[at, :] - LEARNING_RATE * dot3(high_low(m_ref[at, :]), right)
        copy = remote(new_q, new_q, slot, partner)
        copy.start()
        copy.wait_send()
        remote(new_o, new_o, slot, partner).wait_recv()

    @pl.when(core == 1)
    def _():
        right = high_low(m_ref[...])
        for i in range(3):
            at = slice(i * BLK, (i + 1) * BLK)
            new_o[at, :] = new_o[at, :] - LEARNING_RATE * dot3(
                high_low(p_s[at, :]), right, ((1,), (1,))
            )
        copy = remote(new_o, new_o, slot, partner)
        copy.start()
        copy.wait_send()
        remote(new_q, new_q, slot, partner).wait_recv()

    for copy in pending:
        copy.wait_send()


COPIES = 80


def per_device(*args):
    hbm = pl.BlockSpec(memory_space=pl.ANY)
    vmem = pl.BlockSpec(memory_space=pltpu.VMEM)
    smem = pl.BlockSpec(memory_space=pltpu.SMEM)

    def v(shape, dtype=F32):
        return pltpu.VMEM(shape, dtype)

    return pl.pallas_call(
        kernel,
        out_shape=(
            jax.ShapeDtypeStruct((BIG, SMALL), F32),
            jax.ShapeDtypeStruct((SMALL, BIG), F32),
        ),
        in_specs=[hbm] * 4 + [smem] + [hbm] * 4 + [vmem] * 2,
        out_specs=(vmem, vmem),
        scratch_shapes=[
            v((1024, BIG), BF16), v((1024, SMALL), BF16), v((1024, BIG), BF16), v((1024, SMALL), BF16),
            v((BIG, BIG)), v((SMALL, SMALL)),
            v((4, BLK, SMALL)), v((4, BLK, SMALL)), v((4, BLK, SMALL)),
            v((4, BLK, SMALL)), v((BLK, SMALL)), v((4, 32, SMALL)), v((32, SMALL)), v((8, 8, SMALL)),
            v((BIG, SMALL)),
            v((7, 16, BLK), BF16), v((7, 16, BLK), BF16), v((4, 7, 32, BLK), BF16),
            v((4, BLK, BLK)), v((4, BLK, BLK)), v((BLK, BLK)), v((8, 32, BLK)), v((16, BLK, BLK)),
            v((8, BLK)), v((4, 4, 8, 2, 8, BLK)),
            v((BIG, BIG)), v((BIG, BIG)), v((BIG, BIG), BF16), v((BIG, BIG), BF16),
            v((SMALL, SMALL)), v((SMALL, SMALL)), v((SMALL, SMALL), BF16), v((SMALL, SMALL), BF16),
            v((BIG, SMALL)),
            pltpu.SemaphoreType.DMA((6,)),
            pltpu.SemaphoreType.DMA((COPIES,)),
            pltpu.SemaphoreType.DMA((COPIES,)),
        ],
        compiler_params=pltpu.CompilerParams(
            collective_id=0, has_side_effects=True, vmem_limit_bytes=64000000
        ),
    )(*args)


def solution(mesh):
    return jax.shard_map(
        per_device,
        mesh=mesh,
        in_specs=(P(("dp", "own"), None),) * 4
        + (P(("dp", "own")),)
        + (P(),) * 4
        + (P("dp", "own"),) * 2,
        out_specs=(P(), P()),
        check_vma=False,
    )
```

time: 784 us -> 77.8 us (0.10); the launches traced: 769 us -> 77.7 us
  waiting for transfers between devices: 412 us -> 0 us
  blocking collectives: 256 us -> 0 us
  Pallas kernels: 0 us -> 74 us
  matrix products: 54.3 us -> 0 us
  between operations: 14.4 us -> 0.65 us
  other arithmetic: 10.8 us -> 0 us
  loops' own time: 10 us -> 0 us
  local copies, waits for them, and re-layouts: 11.1 us -> 3.02 us
    psum x2 -> x0, waiting for transfers between devices: 412 us -> none  [the longest x1 277 us: per_device(): lax.psum((outer_sum(picked[0]), outer_sum(picked[1]), outer_sum(picked[2]...]
    all_gather x4 -> x0, blocking collectives: 256 us -> none  [the longest x1 122 us: per_device(): lax.all_gather(wide_o, 'dp', axis=0, tiled=True)]
    pallas_call x0 -> x1, Pallas kernels: none -> 74 us  [per_device(): pl.pallas_call(kernel, out_shape=(jax.ShapeDtypeStruct((BIG, SMALL), F32)...]
    dot_general x26 -> x0, matrix products: 54.3 us -> none  [the longest x8 25 us: newton(): product = jnp.dot(matrix, approx, precision=lax.Precision.HIGHEST)]
    another operation x4 -> x0, loops' own time: 10 us -> none  [per_device(): lax.cond(own_index == owner_root, newton, jnp.zeros_like, factors[factor_...]
  transfers between devices with their start and end apart: 2 -> 0, of which waited for: 2 -> 0; matrix products, arithmetic and copies ran while one was open for 0% -> 0% of each run, Pallas kernels for 0% -> 0%
where the time goes in v1:
time: 77.8 us; the launch traced here: 77.7 us
  Pallas kernels  74 us (95%)
  local copies, waits for them, and re-layouts  3.02 us (4%)
    pallas_call x1, Pallas kernels, per_device(): pl.pallas_call(kernel, out_shape=(jax.ShapeDtypeStruct((BIG, SMALL), F32)...  74 us
    unnamed x4, local copies, waits for them, and re-layouts  3.02 us

profile of v1, /device:TPU:1, one launch (start us, length us, event | category | flops | bytes accessed | tf_op | source)
XLA Modules:
  0.0 77.7 jit_solution(16706554480755787543)
XLA Ops:
  0.6 74.0 %shard_map.122 = (f32[512,384]{1,0:T(8,128)}, f32[384,512]{1,0:T(8,128)}) custom-call(bf16[1024,512]{1,0:T(8,128)(2,1)} %acts_q.1, bf16[1024,384]{1,0:T(8,128)(2,1)} %grads_q.1, bf16[1024,384]{1,0:T(8,128)(2,1)} %acts_o.1, bf16[1024,512]{1,0:T(8,128)(2,1)} %grads_o.1, s32[16]{0:T(128)} %rows_ref.1, f32[512,512]{1,0:T(8,128)} %start_aq.1, ...), custom_call_target="tpu_custom_call" | custom-call | tf_op jit(solution)/shard_map/pallas_call | solution.py:473
  74.6 0.0 copy-start
  74.7 2.1 %copy.15 = f32[512,384]{1,0:T(8,128)} copy(f32[512,384]{1,0:T(8,128)} %get-tuple-element.4) | data formatting | bytes 1572864
  76.8 0.0 copy-done
  76.8 0.9 %copy.16 = f32[384,512]{1,0:T(8,128)} copy(f32[384,512]{1,0:T(8,128)S(1)} %copy-done) | data formatting | bytes 1572864
Async XLA Ops:
  74.6 2.1 %copy-start = (f32[384,512]{1,0:T(8,128)S(1)}, f32[384,512]{1,0:T(8,128)}, u32[]{:S(2)}) copy-start(f32[384,512]{1,0:T(8,128)} %get-tuple-element.5) | copy-start | bytes 2359300

commit v2 on v1

--- a/solution.py
+++ b/solution.py
@@ -97,9 +97,9 @@
     start_aq, start_gq, start_ao, start_go, wq_ref, wo_ref,
     new_q, new_o,
     mine_b, mine_s, oth_b, oth_s, st_b, st_s,
-    g_send, g_mine, g_core, g_y, g_ysum, g_x, g_xsum, g_z, g_full,
+    g_send, g_mine, g_core, g_part, g_relay, g_got, g_sum, g_x, g_xsum, g_z, g_full,
     s_send, s_core, s_all,
-    c_part, c_y, c_ysum, c_z, c_blocks,
+    c_part, c_relay, c_got, c_ysum, c_z, c_blocks,
     w_send, w_all,
     e_b, p_b, eb_b, pb_b, e_s, p_s, eb_s, pb_s, m_ref,
     in_sem, send_sem, recv_sem,
@@ -151,11 +151,58 @@
 
     pending = []
 
-    def send(src, dst, slot, peer):
-        copy = remote(src, dst, slot, peer)
+    def send(src, dst, peer):
+        copy = remote(src, dst, len(pending), peer)
         copy.start()
         pending.append(copy)
         return copy
+
+    def land(copies):
+        for copy in copies:
+            copy.wait_recv()
+
+    def spread(view, peers):
+        return [send(view, view, peer) for peer in peers]
+
+    class Scatter:
+        def __init__(self, buf, relay, got, me, peer):
+            self.buf, self.relay, self.got, self.me, self.peer = buf, relay, got, me, peer
+            far, self.after, self.before = (lax.rem(me + d, 4) for d in (2, 1, 3))
+            self.first = [
+                send(buf.at[far, 0], relay.at[0], peer[1]),
+                send(buf.at[far, 1], relay.at[1], peer[3]),
+            ]
+            self.rest = [
+                send(buf.at[self.after, 1], got.at[0, 1], peer[1]),
+                send(buf.at[self.before, 0], got.at[1, 0], peer[3]),
+            ]
+
+        def forward(self):
+            for part, (chunk, peer) in enumerate(((self.after, self.peer[1]), (self.before, self.peer[3]))):
+                self.first[part].wait_recv()
+                self.buf[chunk, part] = self.buf[chunk, part] + self.relay[part]
+                self.rest.append(send(self.buf.at[chunk, part], self.got.at[part, part], peer))
+
+        def sums(self):
+            land(self.rest)
+            return [(self.buf[self.me, p] + self.got[0, p]) + self.got[1, p] for p in range(2)]
+
+    class Gather:
+        def __init__(self, view, me, peer):
+            self.view, self.peer = view, peer
+            self.after, self.before = lax.rem(me + 1, 4), lax.rem(me + 3, 4)
+            mine = [view(me, 0), view(me, 1)]
+            self.first = [send(mine[0], mine[0], peer[1]), send(mine[1], mine[1], peer[3])]
+            self.rest = [send(mine[1], mine[1], peer[1]), send(mine[0], mine[0], peer[3])]
+
+        def forward(self):
+            for part, (chunk, peer) in enumerate(((self.before, self.peer[1]), (self.after, self.peer[3]))):
+                self.first[part].wait_recv()
+                view = self.view(chunk, part)
+                self.rest.append(send(view, view, peer))
+
+        def finish(self):
+            land(self.rest)
 
     w_send[...] = jnp.zeros_like(w_send)
 
@@ -195,167 +242,134 @@
 
     pl.semaphore_wait(barrier, 14)
 
-    slot = 0
-    s_copy = send(s_send, s_core, slot, partner)
-    slot += 1
-    w_copy = send(w_send, w_all.at[x, y, z, core], slot, partner)
-    slot += 1
+    s_copy = send(s_send, s_core, partner)
+    w_copy = send(w_send, w_all.at[x, y, z, core], partner)
 
     g_copies = []
-    for d in (1, 2, 3, 0):
+    for d in (2, 1, 3, 0):
         c = lax.rem(y + d, 4)
         cols = pl.ds(pl.multiple_of(c * BLK, BLK), BLK)
         g_send[d] = dot(oth_b[:, cols], oth_s[...], ((0,), (0,)))
-        g_copies.append(send(g_send.at[d], g_core.at[d], slot, partner))
-        slot += 1
+        g_copies.append(send(g_send.at[d], g_core.at[d], partner))
+        if d == 2:
+            s_copy.wait_recv()
+            for b in range(7):
+                s_all[x, b, pl.ds(pl.multiple_of((1 - core) * 16, 16), 16), :] = s_core[b]
+            s_gather = Gather(lambda i, p: s_all.at[i, pl.ds(4 * p, 4 - p)], x, x_peer)
         g_mine[d] = dot(mine_b[:, cols], mine_s[...], ((0,), (0,)))
 
-    s_copy.wait_recv()
-    for b in range(7):
-        s_all[x, b, pl.ds(pl.multiple_of((1 - core) * 16, 16), 16), :] = s_core[b]
-    s_copies = []
-    for d in (1, 2, 3):
-        s_copies.append(send(s_all.at[x], s_all.at[x], slot, x_peer[d]))
-        slot += 1
-
-    gy_copies = []
-    for index, d in enumerate((1, 2, 3, 0)):
+    w_copy.wait_recv()
+    w_copies = spread(w_all.at[x, y, z], z_peer[1:])
+    s_gather.forward()
+
+    for index, d in enumerate((2, 1, 3, 0)):
+        c = lax.rem(y + d, 4)
         g_copies[index].wait_recv()
         total = g_mine[d] + g_core[d]
-        if d == 0:
-            g_y[y] = total
-        else:
-            g_mine[d] = total
-            gy_copies.append(send(g_mine.at[d], g_y.at[y], slot, y_peer[d]))
-            slot += 1
-
-    w_copy.wait_recv()
-    w_copies = []
-    for d in range(1, 8):
-        w_copies.append(send(w_all.at[x, y, z], w_all.at[x, y, z], slot, z_peer[d]))
-        slot += 1
-
-    for copy in s_copies:
-        copy.wait_recv()
-    cy_copies = []
-    for d in (1, 2, 3, 0):
-        block = x * 4 + lax.rem(y + d, 4)
+        for b in range(4):
+            g_part[0, c, b // 2, b % 2] = total[b * 32 : b * 32 + 16]
+            g_part[1, b, c // 2, lax.rem(c, 2)] = total[b * 32 + 16 : b * 32 + 32]
+    g_scatter = [
+        Scatter(g_part.at[0], g_relay.at[0], g_got.at[0], y, y_peer),
+        Scatter(g_part.at[1], g_relay.at[1], g_got.at[1], x, x_peer),
+    ]
+
+    s_gather.finish()
+    for d in (2, 1, 3, 0):
+        c = lax.rem(y + d, 4)
+        block = x * 4 + c
         left = lookup(block, [i for i, _ in PAIRS])
         right = lookup(block, [j for _, j in PAIRS])
         lhs = s_all[:, left].reshape(128, BLK)
         rhs = s_all[:, right].reshape(128, BLK)
         value = dot(lhs, rhs, ((0,), (0,)))
-        if d == 0:
-            c_y[y] = value
-        else:
-            c_part[d] = value
-            cy_copies.append(send(c_part.at[d], c_y.at[y], slot, y_peer[d]))
-            slot += 1
-
-    for copy in w_copies:
-        copy.wait_recv()
-    w_copies = []
-    for d in (1, 2, 3):
-        w_copies.append(send(w_all.at[x, y], w_all.at[x, y], slot, y_peer[d]))
-        slot += 1
-
-    for copy in cy_copies:
-        copy.wait_recv()
-    c_ysum[...] = (c_y[0] + c_y[1]) + (c_y[2] + c_y[3])
+        c_part[c, 0] = value[0:64]
+        c_part[c, 1] = value[64:128]
+    c_scatter = Scatter(c_part, c_relay, c_got, y, y_peer)
+    g_scatter[0].forward()
+    g_scatter[1].forward()
+    c_scatter.forward()
+
+    for p, value in enumerate(c_scatter.sums()):
+        c_ysum[p * 64 : (p + 1) * 64, :] = value
     cz_copies = []
     for d in range(1, 8):
         rows = pl.ds(pl.multiple_of(lax.rem(z + d, 4) * 32, 32), 32)
-        cz_copies.append(send(c_ysum.at[rows], c_z.at[z], slot, z_peer[d]))
-        slot += 1
+        cz_copies.append(send(c_ysum.at[rows], c_z.at[z], z_peer[d]))
     c_z[z] = c_ysum[pl.ds(pl.multiple_of(own * 32, 32), 32), :]
 
-    for copy in gy_copies:
-        copy.wait_recv()
-    g_ysum[...] = (g_y[0] + g_y[1]) + (g_y[2] + g_y[3])
+    for h in range(2):
+        for p, value in enumerate(g_scatter[h].sums()):
+            g_sum[h, p] = value
     gx_copies = []
     for d in (1, 2, 3):
-        rows = pl.ds(pl.multiple_of(lax.rem(x + d, 4) * 32, 32), 32)
-        gx_copies.append(send(g_ysum.at[rows], g_x.at[x], slot, x_peer[d]))
-        slot += 1
-    g_x[x] = g_ysum[pl.ds(pl.multiple_of(x * 32, 32), 32), :]
-
-    for copy in w_copies:
-        copy.wait_recv()
-    w_copies = []
-    for d in (1, 2, 3):
-        w_copies.append(send(w_all.at[x], w_all.at[x], slot, x_peer[d]))
-        slot += 1
-
-    my_block = x * 4 + y
-    for copy in cz_copies:
-        copy.wait_recv()
+        to = lax.rem(x + d, 4)
+        gx_copies.append(send(g_sum.at[0, to // 2, lax.rem(to, 2)], g_x.at[0, x], x_peer[d]))
+        to = lax.rem(y + d, 4)
+        gx_copies.append(send(g_sum.at[1, to // 2, lax.rem(to, 2)], g_x.at[1, y], y_peer[d]))
+    g_x[0, x] = g_sum[0, x // 2, lax.rem(x, 2)]
+    g_x[1, y] = g_sum[1, y // 2, lax.rem(y, 2)]
+
+    land(gx_copies)
+    for h in range(2):
+        g_xsum[h * 16 : (h + 1) * 16, :] = (g_x[h, 0] + g_x[h, 1]) + (g_x[h, 2] + g_x[h, 3])
+    gz_copies = []
+    for d in range(1, 8):
+        rows = pl.ds(pl.multiple_of(lax.rem(z + d, 4) * 8, 8), 8)
+        gz_copies.append(send(g_xsum.at[rows], g_z.at[z], z_peer[d]))
+    g_z[z] = g_xsum[pl.ds(pl.multiple_of(own * 8, 8), 8), :]
+
+    land(w_copies)
+    w_copies = spread(w_all.at[x, y, pl.ds(0, 4)], y_peer[1:])
+    w_copies += spread(w_all.at[x, y, pl.ds(4, 4)], x_peer[1:])
+
+    land(cz_copies)
     total = c_z[0]
     for k in range(1, 8):
         total = total + c_z[k]
-    c_rows = pl.ds(pl.multiple_of(own * 32, 32), 32)
-    c_blocks[my_block, c_rows, :] = total
-    cag_copies = []
-    for d in (1, 7, 6):
-        view = c_blocks.at[my_block, c_rows]
-        cag_copies.append(send(view, view, slot, z_peer[d]))
-        slot += 1
-
-    for copy in gx_copies:
-        copy.wait_recv()
-    g_xsum[...] = (g_x[0] + g_x[1]) + (g_x[2] + g_x[3])
-    gz_copies = []
-    for d in range(1, 8):
-        rows = pl.ds(pl.multiple_of(lax.rem(z + d, 4) * 8, 8), 8)
-        gz_copies.append(send(g_xsum.at[rows], g_z.at[z], slot, z_peer[d]))
-        slot += 1
-    g_z[z] = g_xsum[pl.ds(pl.multiple_of(own * 8, 8), 8), :]
-
-    for copy in cag_copies:
-        copy.wait_recv()
-    cag_copies = []
-    for d in (1, 2, 3):
-        view = c_blocks.at[my_block]
-        cag_copies.append(send(view, view, slot, y_peer[d]))
-        slot += 1
-
-    for copy in gz_copies:
-        copy.wait_recv()
+    c_view = (x, y, own // 2, pl.ds(pl.multiple_of(lax.rem(own, 2) * 32, 32), 32))
+    c_blocks[c_view] = total
+    cag_copies = spread(c_blocks.at[c_view], [z_peer[d] for d in (1, 7, 6)])
+
+    land(w_copies)
+    w_gather = [
+        Gather(lambda i, p: w_all.at[i, pl.ds(2 * p, 2), pl.ds(0, 4)], x, x_peer),
+        Gather(lambda i, p: w_all.at[pl.ds(2 * p, 2), i, pl.ds(4, 4)], y, y_peer),
+    ]
+
+    land(cag_copies)
+    cag_copies = spread(c_blocks.at[x, y, 0], y_peer[1:]) + spread(c_blocks.at[x, y, 1], x_peer[1:])
+
+    land(gz_copies)
     total = g_z[0]
     for k in range(1, 8):
         total = total + g_z[k]
-    base = y * 128 + x * 32
-    g_rows = pl.ds(pl.multiple_of(base + own * 8, 8), 8)
-    g_full[g_rows, :] = total
-    gag_copies = []
-    for d in (1, 7, 6):
-        gag_copies.append(send(g_full.at[g_rows], g_full.at[g_rows], slot, z_peer[d]))
-        slot += 1
-
-    for copy in cag_copies:
-        copy.wait_recv()
-    cag_copies = []
-    for d in (1, 2, 3):
-        view = c_blocks.at[pl.ds(x * 4, 4)]
-        cag_copies.append(send(view, view, slot, x_peer[d]))
-        slot += 1
-
-    for copy in gag_copies:
-        copy.wait_recv()
-    gag_copies = []
-    g_rows = pl.ds(pl.multiple_of(base, 32), 32)
-    for d in (1, 2, 3):
-        gag_copies.append(send(g_full.at[g_rows], g_full.at[g_rows], slot, x_peer[d]))
-        slot += 1
-    for copy in gag_copies:
-        copy.wait_recv()
-    gag_copies = []
-    g_rows = pl.ds(pl.multiple_of(y * 128, 128), 128)
-    for d in (1, 2, 3):
-        gag_copies.append(send(g_full.at[g_rows], g_full.at[g_rows], slot, y_peer[d]))
-        slot += 1
-
-    for copy in w_copies:
-        copy.wait_recv()
+    g_view = (y, x, pl.ds(pl.multiple_of(own * 8, 8), 8))
+    g_full[g_view] = total
+    gag_copies = spread(g_full.at[g_view], [z_peer[d] for d in (1, 7, 6)])
+
+    w_gather[0].forward()
+    w_gather[1].forward()
+
+    land(cag_copies)
+    c_gather = [
+        Gather(lambda i, p: c_blocks.at[i, pl.ds(2 * p, 2), 0], x, x_peer),
+        Gather(lambda i, p: c_blocks.at[pl.ds(2 * p, 2), i, 1], y, y_peer),
+    ]
+
+    land(gag_copies)
+    gag_copies = spread(g_full.at[y, x, pl.ds(0, 16)], x_peer[1:])
+    gag_copies += spread(g_full.at[y, x, pl.ds(16, 16)], y_peer[1:])
+    c_gather[0].forward()
+    c_gather[1].forward()
+    land(gag_copies)
+    g_gather = [
+        Gather(lambda i, p: g_full.at[i, pl.ds(2 * p, 2), pl.ds(0, 16)], y, y_peer),
+        Gather(lambda i, p: g_full.at[pl.ds(2 * p, 2), i, pl.ds(16, 16)], x, x_peer),
+    ]
+
+    w_gather[0].finish()
+    w_gather[1].finish()
 
     @pl.when(core == 0)
     def _():
@@ -388,8 +402,8 @@
 
     fetch(start_aq, st_b, 4).wait()
     fetch(start_gq, st_s, 5).wait()
-    for copy in cag_copies:
-        copy.wait_recv()
+    c_gather[0].finish()
+    c_gather[1].finish()
 
     def factor(n, offset, st_ref, e_ref, p_ref):
         count = n // BLK
@@ -397,7 +411,8 @@
         squares = jnp.zeros((1, 1), F32)
         for i in range(count):
             for j in range(i, count):
-                block = c_blocks[where[(i + offset, j + offset)]] * (1.0 / SAMPLES)
+                position = where[(i + offset, j + offset)]
+                block = c_blocks[position // 4, position % 4].reshape(BLK, BLK) * (1.0 / SAMPLES)
                 for a, b, value in ((i, j, block), (j, i, block.T)) if i != j else ((i, j, block),):
                     at = (slice(a * BLK, (a + 1) * BLK), slice(b * BLK, (b + 1) * BLK))
                     mixed = DECAY * st_ref[at] + (1.0 - DECAY) * value
@@ -415,6 +430,8 @@
             p_ref[at, :] = scale * (one + rest)
 
     factor(BIG, 0, st_b, e_b, p_b)
+    g_gather[0].forward()
+    g_gather[1].forward()
     factor(SMALL, 4, st_s, e_s, p_s)
 
     def iterate(step, carry):
@@ -424,12 +441,17 @@
 
     lax.fori_loop(0, 3, iterate, 0)
 
-    for copy in gag_copies:
-        copy.wait_recv()
-    grad = high_low(g_full[...] * (1.0 / TOKENS))
+    g_gather[0].finish()
+    g_gather[1].finish()
+    grad = high_low(g_full[...].reshape(BIG, SMALL) * (1.0 / TOKENS))
     for i in range(4):
         at = slice(i * BLK, (i + 1) * BLK)
         m_ref[at, :] = dot3(high_low(p_b[at, :]), grad)
+    slot = len(pending)
+
+    def rows_of(ref, i):
+        view = ref.at[pl.ds(i * BLK, BLK)]
+        return remote(view, view, slot + i, partner)
 
     @pl.when(core == 0)
     def _():
@@ -437,10 +459,11 @@
         for i in range(4):
             at = slice(i * BLK, (i + 1) * BLK)
             new_q[at, :] = new_q[at, :] - LEARNING_RATE * dot3(high_low(m_ref[at, :]), right)
-        copy = remote(new_q, new_q, slot, partner)
-        copy.start()
-        copy.wait_send()
-        remote(new_o, new_o, slot, partner).wait_recv()
+            rows_of(new_q, i).start()
+        for i in range(4):
+            rows_of(new_q, i).wait_send()
+        for i in range(3):
+            rows_of(new_o, i).wait_recv()
 
     @pl.when(core == 1)
     def _():
@@ -450,16 +473,17 @@
             new_o[at, :] = new_o[at, :] - LEARNING_RATE * dot3(
                 high_low(p_s[at, :]), right, ((1,), (1,))
             )
-        copy = remote(new_o, new_o, slot, partner)
-        copy.start()
-        copy.wait_send()
-        remote(new_q, new_q, slot, partner).wait_recv()
+            rows_of(new_o, i).start()
+        for i in range(3):
+            rows_of(new_o, i).wait_send()
+        for i in range(4):
+            rows_of(new_q, i).wait_recv()
 
     for copy in pending:
         copy.wait_send()
 
 
-COPIES = 80
+COPIES = 128
 
 
 def per_device(*args):
@@ -482,10 +506,12 @@
             v((1024, BIG), BF16), v((1024, SMALL), BF16), v((1024, BIG), BF16), v((1024, SMALL), BF16),
             v((BIG, BIG)), v((SMALL, SMALL)),
             v((4, BLK, SMALL)), v((4, BLK, SMALL)), v((4, BLK, SMALL)),
-            v((4, BLK, SMALL)), v((BLK, SMALL)), v((4, 32, SMALL)), v((32, SMALL)), v((8, 8, SMALL)),
-            v((BIG, SMALL)),
+            v((2, 4, 2, 2, 16, SMALL)), v((2, 2, 2, 16, SMALL)), v((2, 2, 2, 2, 16, SMALL)),
+            v((2, 2, 2, 16, SMALL)), v((2, 4, 16, SMALL)), v((32, SMALL)), v((8, 8, SMALL)),
+            v((4, 4, 32, SMALL)),
             v((7, 16, BLK), BF16), v((7, 16, BLK), BF16), v((4, 7, 32, BLK), BF16),
-            v((4, BLK, BLK)), v((4, BLK, BLK)), v((BLK, BLK)), v((8, 32, BLK)), v((16, BLK, BLK)),
+            v((4, 2, 64, BLK)), v((2, 64, BLK)), v((2, 2, 64, BLK)),
+            v((BLK, BLK)), v((8, 32, BLK)), v((4, 4, 2, 64, BLK)),
             v((8, BLK)), v((4, 4, 8, 2, 8, BLK)),
             v((BIG, BIG)), v((BIG, BIG)), v((BIG, BIG), BF16), v((BIG, BIG), BF16),
             v((SMALL, SMALL)), v((SMALL, SMALL)), v((SMALL, SMALL), BF16), v((SMALL, SMALL), BF16),

time: 77.8 us -> 69.4 us (0.89)
  Pallas kernels: 74 us -> 65.6 us
    pallas_call x1, Pallas kernels: 74 us -> 65.6 us  [per_device(): pl.pallas_call(kernel, out_shape=(jax.ShapeDtypeStruct((BIG, SMALL), F32)...]
where the time goes in v2:
time: 69.4 us; the launch traced here: 69.2 us
  Pallas kernels  65.6 us (95%)
  local copies, waits for them, and re-layouts  3.02 us (4%)
    pallas_call x1, Pallas kernels, per_device(): pl.pallas_call(kernel, out_shape=(jax.ShapeDtypeStruct((BIG, SMALL), F32)...  65.6 us
    unnamed x4, local copies, waits for them, and re-layouts  3.02 us

profile of v2, /device:TPU:1, one launch (start us, length us, event | category | flops | bytes accessed | tf_op | source)
XLA Modules:
  0.0 69.2 jit_solution(5195182140917239221)
XLA Ops:
  0.6 65.6 %shard_map.122 = (f32[512,384]{1,0:T(8,128)}, f32[384,512]{1,0:T(8,128)}) custom-call(bf16[1024,512]{1,0:T(8,128)(2,1)} %acts_q.1, bf16[1024,384]{1,0:T(8,128)(2,1)} %grads_q.1, bf16[1024,384]{1,0:T(8,128)(2,1)} %acts_o.1, bf16[1024,512]{1,0:T(8,128)(2,1)} %grads_o.1, s32[16]{0:T(128)} %rows_ref.1, f32[512,512]{1,0:T(8,128)} %start_aq.1, ...), custom_call_target="tpu_custom_call" | custom-call | tf_op jit(solution)/shard_map/pallas_call | solution.py:497
  66.2 0.0 copy-start
  66.2 2.1 %copy.15 = f32[512,384]{1,0:T(8,128)} copy(f32[512,384]{1,0:T(8,128)} %get-tuple-element.4) | data formatting | bytes 1572864
  68.3 0.0 copy-done
  68.3 0.9 %copy.16 = f32[384,512]{1,0:T(8,128)} copy(f32[384,512]{1,0:T(8,128)S(1)} %copy-done) | data formatting | bytes 1572864
Async XLA Ops:
  66.2 2.1 %copy-start = (f32[384,512]{1,0:T(8,128)S(1)}, f32[384,512]{1,0:T(8,128)}, u32[]{:S(2)}) copy-start(f32[384,512]{1,0:T(8,128)} %get-tuple-element.5) | copy-start | bytes 2359300

commit v3 on v2

--- a/solution.py
+++ b/solution.py
@@ -331,12 +331,6 @@
     c_blocks[c_view] = total
     cag_copies = spread(c_blocks.at[c_view], [z_peer[d] for d in (1, 7, 6)])
 
-    land(w_copies)
-    w_gather = [
-        Gather(lambda i, p: w_all.at[i, pl.ds(2 * p, 2), pl.ds(0, 4)], x, x_peer),
-        Gather(lambda i, p: w_all.at[pl.ds(2 * p, 2), i, pl.ds(4, 4)], y, y_peer),
-    ]
-
     land(cag_copies)
     cag_copies = spread(c_blocks.at[x, y, 0], y_peer[1:]) + spread(c_blocks.at[x, y, 1], x_peer[1:])
 
@@ -347,9 +341,6 @@
     g_view = (y, x, pl.ds(pl.multiple_of(own * 8, 8), 8))
     g_full[g_view] = total
     gag_copies = spread(g_full.at[g_view], [z_peer[d] for d in (1, 7, 6)])
-
-    w_gather[0].forward()
-    w_gather[1].forward()
 
     land(cag_copies)
     c_gather = [
@@ -368,37 +359,11 @@
         Gather(lambda i, p: g_full.at[pl.ds(2 * p, 2), i, pl.ds(16, 16)], x, x_peer),
     ]
 
-    w_gather[0].finish()
-    w_gather[1].finish()
-
-    @pl.when(core == 0)
-    def _():
-        def place(step, carry):
-            wx, wy = step // 4, lax.rem(step, 4)
-            for zh in range(2):
-                for cc in range(2):
-                    row = pl.multiple_of(((zh * 4 + wx) * 4 + wy) * 16 + cc * 8, 8)
-                    for o in range(4):
-                        new_q[pl.ds(row, 8), o * 96 : (o + 1) * 96] = w_all[
-                            wx, wy, zh * 4 + o, cc, :, 0:96
-                        ]
-            return carry
-
-        lax.fori_loop(0, 16, place, 0)
-
-    @pl.when(core == 1)
-    def _():
-        def place(step, carry):
-            zh, wx = step // 4, lax.rem(step, 4)
-            row = pl.multiple_of(step * 48, 8)
-            for o in range(4):
-                parts = [
-                    w_all[wx, wy, zh * 4 + o, cc, 0:6, :] for wy in range(4) for cc in range(2)
-                ]
-                new_o[pl.ds(row, 48), o * BLK : (o + 1) * BLK] = jnp.concatenate(parts, axis=0)
-            return carry
-
-        lax.fori_loop(0, 8, place, 0)
+    land(w_copies)
+    w_gather = [
+        Gather(lambda i, p: w_all.at[i, pl.ds(2 * p, 2), pl.ds(0, 4)], x, x_peer),
+        Gather(lambda i, p: w_all.at[pl.ds(2 * p, 2), i, pl.ds(4, 4)], y, y_peer),
+    ]
 
     fetch(start_aq, st_b, 4).wait()
     fetch(start_gq, st_s, 5).wait()
@@ -433,6 +398,8 @@
     g_gather[0].forward()
     g_gather[1].forward()
     factor(SMALL, 4, st_s, e_s, p_s)
+    w_gather[0].forward()
+    w_gather[1].forward()
 
     def iterate(step, carry):
         newton_step(BIG, e_b, p_b, eb_b, pb_b)
@@ -448,6 +415,38 @@
         at = slice(i * BLK, (i + 1) * BLK)
         m_ref[at, :] = dot3(high_low(p_b[at, :]), grad)
     slot = len(pending)
+
+    w_gather[0].finish()
+    w_gather[1].finish()
+
+    @pl.when(core == 0)
+    def _():
+        def place(step, carry):
+            wx, wy = step // 4, lax.rem(step, 4)
+            for zh in range(2):
+                for cc in range(2):
+                    row = pl.multiple_of(((zh * 4 + wx) * 4 + wy) * 16 + cc * 8, 8)
+                    for o in range(4):
+                        new_q[pl.ds(row, 8), o * 96 : (o + 1) * 96] = w_all[
+                            wx, wy, zh * 4 + o, cc, :, 0:96
+                        ]
+            return carry
+
+        lax.fori_loop(0, 16, place, 0)
+
+    @pl.when(core == 1)
+    def _():
+        def place(step, carry):
+            zh, wx = step // 4, lax.rem(step, 4)
+            row = pl.multiple_of(step * 48, 8)
+            for o in range(4):
+                parts = [
+                    w_all[wx, wy, zh * 4 + o, cc, 0:6, :] for wy in range(4) for cc in range(2)
+                ]
+                new_o[pl.ds(row, 48), o * BLK : (o + 1) * BLK] = jnp.concatenate(parts, axis=0)
+            return carry
+
+        lax.fori_loop(0, 8, place, 0)
 
     def rows_of(ref, i):
         view = ref.at[pl.ds(i * BLK, BLK)]

time: 69.4 us -> 70.8 us (1.020)
  Pallas kernels: 65.6 us -> 67 us
    pallas_call x1, Pallas kernels: 65.6 us -> 67 us  [per_device(): pl.pallas_call(kernel, out_shape=(jax.ShapeDtypeStruct((BIG, SMALL), F32)...]
where the time goes in v3:
time: 70.8 us; the launch traced here: 70.6 us
  Pallas kernels  67 us (95%)
  local copies, waits for them, and re-layouts  3.02 us (4%)
    pallas_call x1, Pallas kernels, per_device(): pl.pallas_call(kernel, out_shape=(jax.ShapeDtypeStruct((BIG, SMALL), F32)...  67 us
    unnamed x4, local copies, waits for them, and re-layouts  3.02 us

profile of v3, /device:TPU:1, one launch (start us, length us, event | category | flops | bytes accessed | tf_op | source)
XLA Modules:
  0.0 70.6 jit_solution(1265808332618886868)
XLA Ops:
  0.6 67.0 %shard_map.122 = (f32[512,384]{1,0:T(8,128)}, f32[384,512]{1,0:T(8,128)}) custom-call(bf16[1024,512]{1,0:T(8,128)(2,1)} %acts_q.1, bf16[1024,384]{1,0:T(8,128)(2,1)} %grads_q.1, bf16[1024,384]{1,0:T(8,128)(2,1)} %acts_o.1, bf16[1024,512]{1,0:T(8,128)(2,1)} %grads_o.1, s32[16]{0:T(128)} %rows_ref.1, f32[512,512]{1,0:T(8,128)} %start_aq.1, ...), custom_call_target="tpu_custom_call" | custom-call | tf_op jit(solution)/shard_map/pallas_call | solution.py:496
  67.6 0.0 copy-start
  67.6 2.1 %copy.15 = f32[512,384]{1,0:T(8,128)} copy(f32[512,384]{1,0:T(8,128)} %get-tuple-element.4) | data formatting | bytes 1572864
  69.8 0.0 copy-done
  69.8 0.9 %copy.16 = f32[384,512]{1,0:T(8,128)} copy(f32[384,512]{1,0:T(8,128)S(1)} %copy-done) | data formatting | bytes 1572864
Async XLA Ops:
  67.6 2.1 %copy-start = (f32[384,512]{1,0:T(8,128)S(1)}, f32[384,512]{1,0:T(8,128)}, u32[]{:S(2)}) copy-start(f32[384,512]{1,0:T(8,128)} %get-tuple-element.5) | copy-start | bytes 2359300

commit v4 on v2

--- a/solution.py
+++ b/solution.py
@@ -310,6 +310,10 @@
     g_x[0, x] = g_sum[0, x // 2, lax.rem(x, 2)]
     g_x[1, y] = g_sum[1, y // 2, lax.rem(y, 2)]
 
+    land(w_copies)
+    w_copies = spread(w_all.at[x, y, pl.ds(0, 4)], y_peer[1:])
+    w_copies += spread(w_all.at[x, y, pl.ds(4, 4)], x_peer[1:])
+
     land(gx_copies)
     for h in range(2):
         g_xsum[h * 16 : (h + 1) * 16, :] = (g_x[h, 0] + g_x[h, 1]) + (g_x[h, 2] + g_x[h, 3])
@@ -320,8 +324,10 @@
     g_z[z] = g_xsum[pl.ds(pl.multiple_of(own * 8, 8), 8), :]
 
     land(w_copies)
-    w_copies = spread(w_all.at[x, y, pl.ds(0, 4)], y_peer[1:])
-    w_copies += spread(w_all.at[x, y, pl.ds(4, 4)], x_peer[1:])
+    w_gather = [
+        Gather(lambda i, p: w_all.at[i, pl.ds(2 * p, 2), pl.ds(0, 4)], x, x_peer),
+        Gather(lambda i, p: w_all.at[pl.ds(2 * p, 2), i, pl.ds(4, 4)], y, y_peer),
+    ]
 
     land(cz_copies)
     total = c_z[0]
@@ -331,11 +337,8 @@
     c_blocks[c_view] = total
     cag_copies = spread(c_blocks.at[c_view], [z_peer[d] for d in (1, 7, 6)])
 
-    land(w_copies)
-    w_gather = [
-        Gather(lambda i, p: w_all.at[i, pl.ds(2 * p, 2), pl.ds(0, 4)], x, x_peer),
-        Gather(lambda i, p: w_all.at[pl.ds(2 * p, 2), i, pl.ds(4, 4)], y, y_peer),
-    ]
+    w_gather[0].forward()
+    w_gather[1].forward()
 
     land(cag_copies)
     cag_copies = spread(c_blocks.at[x, y, 0], y_peer[1:]) + spread(c_blocks.at[x, y, 1], x_peer[1:])
@@ -347,9 +350,6 @@
     g_view = (y, x, pl.ds(pl.multiple_of(own * 8, 8), 8))
     g_full[g_view] = total
     gag_copies = spread(g_full.at[g_view], [z_peer[d] for d in (1, 7, 6)])
-
-    w_gather[0].forward()
-    w_gather[1].forward()
 
     land(cag_copies)
     c_gather = [

time: 69.4 us -> 68.8 us (level)
  no operation moved by 1% of the time
where the time goes in v4:
time: 68.8 us; the launch traced here: 68.7 us
  Pallas kernels  65 us (94%)
  local copies, waits for them, and re-layouts  3.02 us (4%)
    pallas_call x1, Pallas kernels, per_device(): pl.pallas_call(kernel, out_shape=(jax.ShapeDtypeStruct((BIG, SMALL), F32)...  65 us
    unnamed x4, local copies, waits for them, and re-layouts  3.02 us

profile of v4, /device:TPU:1, one launch (start us, length us, event | category | flops | bytes accessed | tf_op | source)
XLA Modules:
  0.0 68.7 jit_solution(5081026560312933065)
XLA Ops:
  0.6 65.0 %shard_map.122 = (f32[512,384]{1,0:T(8,128)}, f32[384,512]{1,0:T(8,128)}) custom-call(bf16[1024,512]{1,0:T(8,128)(2,1)} %acts_q.1, bf16[1024,384]{1,0:T(8,128)(2,1)} %grads_q.1, bf16[1024,384]{1,0:T(8,128)(2,1)} %acts_o.1, bf16[1024,512]{1,0:T(8,128)(2,1)} %grads_o.1, s32[16]{0:T(128)} %rows_ref.1, f32[512,512]{1,0:T(8,128)} %start_aq.1, ...), custom_call_target="tpu_custom_call" | custom-call | tf_op jit(solution)/shard_map/pallas_call | solution.py:497
  65.6 0.0 copy-start
  65.6 2.1 %copy.15 = f32[512,384]{1,0:T(8,128)} copy(f32[512,384]{1,0:T(8,128)} %get-tuple-element.4) | data formatting | bytes 1572864
  67.8 0.0 copy-done
  67.8 0.9 %copy.16 = f32[384,512]{1,0:T(8,128)} copy(f32[384,512]{1,0:T(8,128)S(1)} %copy-done) | data formatting | bytes 1572864
Async XLA Ops:
  65.6 2.1 %copy-start = (f32[384,512]{1,0:T(8,128)S(1)}, f32[384,512]{1,0:T(8,128)}, u32[]{:S(2)}) copy-start(f32[384,512]{1,0:T(8,128)} %get-tuple-element.5) | copy-start | bytes 2359300
